TPU v7x, 32 devices: a whole 2x2x4 slice. The times are simulated.
32 devices in a mesh: row: 8 (over y, x, core), col: 4 (over z).
Axes of the slice: x: 2, y: 2, z: 4, core: 2. Of those that a mesh axis runs over, the one named last changes fastest.
Arguments:
- start_modes: float32 [32, 131072], P(None, ('row', 'col')), may hold values from -6 to 6
- energies: float32 [131072], P(('row', 'col')), may hold values from -0.5 to 0.5
- coupling: float32 [2048, 20, 4096], P('row', 'col'), may hold values from -0.078125 to 0.078125
- pattern: int32 [2048, 20], P('row', 'col'), may hold values from 0 to 2047, as said below
Outputs:
- filtered: float32 [32, 131072], P(None, ('row', 'col'))
- previous: float32 [32, 131072], P(None, ('row', 'col'))
Inputs may be any that keep to these rules, and one draw needn't show every extreme that they name: In block row i, the 5 entries pattern[i, c * 5] to pattern[i, c * 5 + 4] are distinct block columns j with (j // 64) % 4 == c.
All inputs are finite; a program needn't handle non-finite values.
Results may differ from a plain program's by a relative error of at most 0.0001.
Values sent between devices are 32-bit elements; how exact they have to be, the bound alone decides.
A program may use at most 192 MiB of HBM per device.

v0:
```python
import functools

import jax
import jax.numpy as jnp
from jax import lax
from jax.experimental import pallas as pl
from jax.experimental.pallas import tpu as pltpu
from jax.sharding import PartitionSpec as P

BLOCK = 64
DEGREE = 3
LANES = 128


def low_half(shape):
    return lax.broadcasted_iota(jnp.int32, shape, len(shape) - 1) < BLOCK


def split(x):
    high = x.astype(jnp.bfloat16)
    return high, (x - high.astype(jnp.float32)).astype(jnp.bfloat16)


MESH = pl.DeviceIdType.MESH


def filter_kernel(
    slots, n_row, n_col, halves,
    places_ref, start_ref, energies_ref, coupling_ref, filtered_ref, previous_ref,
    c_buf, stage, prepared, gathered, blocks, first_ref, partial, landed,
    c_sem, gather_send, gather_recv, share_send, share_recv,
):
    row, col = lax.axis_index("row"), lax.axis_index("col")
    chips = n_row // 2
    chip, core = row // 2, row % 2
    partner = chip * 2 + (1 - core)
    modes, piece_len = start_ref.shape
    part = modes // halves
    tiles = piece_len // LANES
    per_piece = piece_len // BLOCK
    rows = prepared.shape[0]
    group = min(16, per_piece)
    terms = (start_ref, first_ref, previous_ref, filtered_ref)

    def other_chip(d):
        if chips & (chips - 1):
            return (chip + d) % chips
        place, bit, rest = chip, 1, abs(d)
        while rest:
            if rest % 2:
                place = place + bit * (1 - 2 * (chip // bit % 2))
            bit, rest = 2 * bit, rest // 2
        return place

    def same_core(d):
        return other_chip(d) * 2 + core

    def other_core(d):
        return other_chip(d) * 2 + (1 - core)

    def share_of(k, h):
        return terms[k].at[pl.ds(h * part, part), :]

    barrier = pltpu.get_barrier_semaphore()
    for d in range(1, chips):
        pl.semaphore_signal(barrier, inc=1, device_id=(same_core(d), col), device_id_type=MESH)
    pl.semaphore_signal(barrier, inc=1, device_id=(partner, col), device_id_type=MESH)
    for d in range(1, n_col):
        pl.semaphore_signal(barrier, inc=1, device_id=(row, (col + d) % n_col), device_id_type=MESH)
    pl.semaphore_wait(barrier, chips + n_col - 1)

    def gather_copy(k, h, source, slot, sem, target):
        return pltpu.make_async_remote_copy(
            src_ref=source,
            dst_ref=gathered.at[k, h, slot],
            send_sem=gather_send.at[k, h, sem],
            recv_sem=gather_recv.at[k, h, slot],
            device_id=(target, col),
            device_id_type=MESH,
        )

    def own_copies(k, h):
        source = share_of(k, h)
        return [gather_copy(k, h, source, row, d, same_core(d)) for d in range(1, chips)] + [
            gather_copy(k, h, source, row, 0, partner)
        ]

    def passed_copies(k, h):
        return [
            gather_copy(k, h, gathered.at[k, h, same_core(-d)], same_core(-d), chips + d, partner)
            for d in range(1, chips)
        ]

    def arrival(k, h, slot):
        return gather_copy(k, h, gathered.at[k, h, slot], slot, 0, partner)

    def gather_start(k, h):
        for copy in own_copies(k, h):
            copy.start()
        gathered[k, h, row] = share_of(k, h)[...]

    def gather_finish(k, h):
        for d, copy in enumerate(passed_copies(k, h), 1):
            arrival(k, h, same_core(-d)).wait_recv()
            copy.start()
        arrival(k, h, partner).wait_recv()
        for d in range(1, chips):
            arrival(k, h, other_core(-d)).wait_recv()

    def share_copy(k, h, target):
        return pltpu.make_async_remote_copy(
            src_ref=partial.at[k, h, target],
            dst_ref=landed.at[k, h, col],
            send_sem=share_send.at[k, h, target],
            recv_sem=share_recv.at[k, h, col],
            device_id=(row, target),
            device_id_type=MESH,
        )

    def share_arrival(k, h, origin):
        return pltpu.make_async_remote_copy(
            src_ref=partial.at[k, h, origin],
            dst_ref=landed.at[k, h, origin],
            send_sem=share_send.at[k, h, origin],
            recv_sem=share_recv.at[k, h, origin],
            device_id=(row, origin),
            device_id_type=MESH,
        )

    def compute(k, h, between):
        low = low_half((part, LANES))
        low_picked = low_half((2 * part, LANES))

        def fill(index, carry):
            for t in range(tiles):
                x = gathered[k, h, index, :, t * LANES : (t + 1) * LANES]
                turned = pltpu.roll(x, BLOCK, 1)
                for side, value in enumerate((jnp.where(low, x, turned), jnp.where(low, turned, x))):
                    high, rest = split(value)
                    place = index * (2 * tiles) + 2 * t + side
                    blocks[place, :part, :] = high
                    blocks[place, part:, :] = rest
            return carry

        lax.fori_loop(0, n_row, fill, 0)

        def one_part(d, carry):
            target = (col + d) % n_col

            def some_rows(step, carry):
                first = target * per_piece + step * group
                done = []
                for i in range(group):
                    base = (first + i) * slots
                    picked = [blocks[places_ref[base + s]] for s in range(slots)]
                    sides = [
                        jnp.where(low_picked, picked[2 * q], picked[2 * q + 1]) if 2 * q + 1 < slots else picked[2 * q]
                        for q in range((slots + 1) // 2)
                    ]
                    product = lax.dot_general(
                        jnp.concatenate(sides, axis=1),
                        prepared[first + i],
                        (((1,), (1,)), ((), ())),
                        preferred_element_type=jnp.float32,
                    )
                    total = product[:part] + product[part:]
                    done.append(total + pltpu.roll(total, BLOCK, 1))
                width = group * BLOCK
                wide = [jnp.where(low, done[2 * q], done[2 * q + 1]) for q in range(group // 2)]
                partial[k, h, target, :, pl.ds(pl.multiple_of(step * width, width), width)] = jnp.concatenate(wide, axis=1)
                return carry

            lax.fori_loop(0, per_piece // group, some_rows, 0)
            return carry

        def one_sent(d, carry):
            one_part(d, carry)
            share_copy(k, h, (col + d) % n_col).start()
            return carry

        lax.fori_loop(1, n_col, one_sent, 0)
        between()
        one_part(0, 0)

    def update(k, h):
        for d in range(1, n_col):
            share_arrival(k, h, (col + d) % n_col).wait_recv()
        here = slice(h * part, (h + 1) * part)

        def tile(t, carry):
            at = pl.ds(pl.multiple_of(t * LANES, LANES), LANES)
            total = partial[k, h, col, :, at]
            for d in range(1, n_col):
                total = total + landed[k, h, (col + d) % n_col, :, at]
            total = energies_ref[:, at] * terms[k][here, at] + total
            if k > 0:
                total = 2.0 * total - terms[k - 1][here, at]
            terms[k + 1][here, at] = total
            return carry

        lax.fori_loop(0, tiles, tile, 0)

    for h in range(halves):
        gather_start(0, h)

    chunk = c_buf.shape[2]
    chunks = rows // chunk

    def fetch(index, slot):
        return pltpu.make_async_copy(
            coupling_ref.at[:, pl.ds(pl.multiple_of(index * chunk, chunk), chunk), :], c_buf.at[slot], c_sem.at[slot]
        )

    fetch(0, 0).start()

    def prepare_chunk(index, carry):
        slot = index % 2

        @pl.when(index + 1 < chunks)
        def _():
            fetch(index + 1, 1 - slot).start()

        fetch(index, slot).wait()
        pairs = (slots + 1) // 2
        low = low_half((chunk, LANES))
        for q in range(pairs):
            for p in range(BLOCK // 2):
                lane = slice(p * LANES, (p + 1) * LANES)
                one = c_buf[slot, 2 * q, :, lane]
                one_turned = pltpu.roll(one, BLOCK, 1)
                if 2 * q + 1 < slots:
                    two = c_buf[slot, 2 * q + 1, :, lane]
                    two_turned = pltpu.roll(two, BLOCK, 1)
                else:
                    two = two_turned = jnp.zeros_like(one)
                stage[q, pl.ds(2 * p, chunk, stride=BLOCK + 1), :] = jnp.where(low, one, two_turned)
                stage[q, pl.ds(2 * p + 1, chunk, stride=BLOCK + 1), :] = jnp.where(low, one_turned, two)
        for q in range(pairs):
            for i in range(chunk):
                high, rest = split(stage[q, i * (BLOCK + 1) : i * (BLOCK + 1) + BLOCK, :])
                prepared[index * chunk + i, :BLOCK, q * LANES : (q + 1) * LANES] = high
                prepared[index * chunk + i, BLOCK:, q * LANES : (q + 1) * LANES] = rest
        return carry

    lax.fori_loop(0, chunks, prepare_chunk, 0)

    stages = [(k, h) for k in range(DEGREE) for h in range(halves)]

    def advance(index):
        if index >= 0:
            k, h = stages[index]
            update(k, h)
            if k + 1 < DEGREE:
                gather_start(k + 1, h)

    for index, (k, h) in enumerate(stages):
        gather_finish(k, h)
        compute(k, h, functools.partial(advance, index - 1))
    advance(len(stages) - 1)
    for k in range(DEGREE):
        for h in range(halves):
            for copy in own_copies(k, h) + passed_copies(k, h):
                copy.wait_send()
            for d in range(1, n_col):
                share_copy(k, h, (col + d) % n_col).wait_send()


def shards(start_modes, energies, coupling, pattern):
    n_row, n_col = lax.axis_size("row"), lax.axis_size("col")
    modes, piece_len = start_modes.shape
    per_piece = piece_len // BLOCK
    rows, slots, entries = coupling.shape
    pairs = (slots + 1) // 2
    chunk, halves = 8, 2
    part = modes // halves
    places = (pattern // per_piece // n_col * per_piece + pattern % per_piece).reshape(-1)
    vmem = pl.BlockSpec(memory_space=pltpu.VMEM)
    filtered, previous = pl.pallas_call(
        functools.partial(filter_kernel, slots, n_row, n_col, halves),
        in_specs=[pl.BlockSpec(memory_space=pltpu.SMEM), vmem, vmem, pl.BlockSpec(memory_space=pl.ANY)],
        out_specs=[vmem, vmem],
        out_shape=[jax.ShapeDtypeStruct(start_modes.shape, jnp.float32)] * 2,
        scratch_shapes=[
            pltpu.VMEM((2, slots, chunk, entries), jnp.float32),
            pltpu.VMEM((pairs, chunk * (BLOCK + 1), LANES), jnp.float32),
            pltpu.VMEM((rows, 2 * BLOCK, pairs * LANES), jnp.bfloat16),
            pltpu.VMEM((DEGREE, halves, n_row, part, piece_len), jnp.float32),
            pltpu.VMEM((n_row * per_piece, 2 * part, LANES), jnp.bfloat16),
            pltpu.VMEM((modes, piece_len), jnp.float32),
            pltpu.VMEM((DEGREE, halves, n_col, part, piece_len), jnp.float32),
            pltpu.VMEM((DEGREE, halves, n_col, part, piece_len), jnp.float32),
            pltpu.SemaphoreType.DMA((2,)),
            pltpu.SemaphoreType.DMA((DEGREE, halves, n_row)),
            pltpu.SemaphoreType.DMA((DEGREE, halves, n_row)),
            pltpu.SemaphoreType.DMA((DEGREE, halves, n_col)),
            pltpu.SemaphoreType.DMA((DEGREE, halves, n_col)),
        ],
        compiler_params=pltpu.CompilerParams(collective_id=0, has_side_effects=True, vmem_limit_bytes=67043328),
        name="filter",
    )(places, start_modes, energies.reshape(1, -1), jnp.transpose(coupling, (1, 0, 2)))
    return filtered, previous


def solution(mesh):
    in_specs = (P(None, ("row", "col")), P(("row", "col")), P("row", "col", None), P("row", "col"))
    out_specs = (P(None, ("row", "col")), P(None, ("row", "col")))
    return jax.shard_map(shards, mesh=mesh, in_specs=in_specs, out_specs=out_specs, check_vma=False)
```

profile of v0, /device:TPU:0, one launch (start us, length us, event | category | flops | bytes accessed | tf_op | source)
XLA Modules:
  0.0 190.7 jit_solution(1263393729537366534)
XLA Ops:
  0.6 0.7 fusion.2
  1.3 0.1 copy.6
  1.5 0.8 reshape.10.places_ref
  2.3 184.6 %filter.1 = (f32[32,4096]{1,0:T(8,128)}, f32[32,4096]{1,0:T(8,128)}) custom-call(s32[1280]{0:T(1024)} %reshape.10.places_ref, f32[32,4096]{1,0:T(8,128)} %start_ref.1, f32[1,4096]{1,0:T(1,128)} %bitcast.3, f32[5,256,4096]{2,1,0:T(8,128)} %bitcast.2), custom_call_target="tpu_custom_call" | custom-call | tf_op jit(solution)/shard_map/filter/pallas_call | solution.py:278
  187.0 1.9 copy.9
  188.8 1.9 copy.10
where the time goes:
time: 191 us
  Pallas kernels  185 us (97%)
  local copies, waits for them, and re-layouts  4.68 us (2%)
    pallas_call x1, Pallas kernels, shards(): pl.pallas_call(functools.partial(filter_kernel, slots, n_row, n_col, halv...  185 us

commit v1 on v0

v1 whole, which is shorter than its diff:
```python
import functools

import jax
import jax.numpy as jnp
from jax import lax
from jax.experimental import pallas as pl
from jax.experimental.pallas import tpu as pltpu
from jax.sharding import PartitionSpec as P

BLOCK = 64
DEGREE = 3
LANES = 128
SUBLANES = 8


def low_half(shape):
    return lax.broadcasted_iota(jnp.int32, shape, len(shape) - 1) < BLOCK


def split(x):
    high = x.astype(jnp.bfloat16)
    return high, (x - high.astype(jnp.float32)).astype(jnp.bfloat16)


MESH = pl.DeviceIdType.MESH


def filter_kernel(
    slots, n_row, n_col, halves,
    places_ref, start_ref, energies_ref, coupling_ref, filtered_ref, previous_ref,
    raw, prepared, gathered, blocks, first_ref, partial, landed,
    raw_sem, gather_send, gather_recv, share_send, share_recv,
):
    row, col = lax.axis_index("row"), lax.axis_index("col")
    chips = n_row // 2
    chip, core = row // 2, row % 2
    partner = chip * 2 + (1 - core)
    modes, piece_len = start_ref.shape
    part = modes // halves
    tiles = piece_len // LANES
    per_piece = piece_len // BLOCK
    rows = prepared.shape[0]
    group = min(16, per_piece)
    pairs = (slots + 1) // 2
    terms = (start_ref, first_ref, previous_ref, filtered_ref)
    relay = chips == 4

    def other_chip(d):
        if chips & (chips - 1):
            return (chip + d) % chips
        place, bit, rest = chip, 1, abs(d)
        while rest:
            if rest % 2:
                place = place + bit * (1 - 2 * (chip // bit % 2))
            bit, rest = 2 * bit, rest // 2
        return place

    def same_core(d):
        return other_chip(d) * 2 + core

    def other_core(d):
        return other_chip(d) * 2 + (1 - core)

    def share_of(k, h):
        return terms[k].at[pl.ds(h * part, part), :]

    barrier = pltpu.get_barrier_semaphore()
    for d in range(1, chips):
        pl.semaphore_signal(barrier, inc=1, device_id=(same_core(d), col), device_id_type=MESH)
    pl.semaphore_signal(barrier, inc=1, device_id=(partner, col), device_id_type=MESH)
    for d in (1, n_col - 1):
        pl.semaphore_signal(barrier, inc=1, device_id=(row, (col + d) % n_col), device_id_type=MESH)
    pl.semaphore_wait(barrier, chips + 2)

    def gather_copy(k, h, source, slot, send, recv, target, modes_of=None):
        place = gathered.at[k, h, slot] if modes_of is None else gathered.at[k, h, slot, modes_of, :]
        return pltpu.make_async_remote_copy(
            src_ref=source,
            dst_ref=place,
            send_sem=gather_send.at[k, h, send],
            recv_sem=gather_recv.at[k, h, recv],
            device_id=(target, col),
            device_id_type=MESH,
        )

    def own_copies(k, h):
        source = share_of(k, h)
        reach = range(1, 3) if relay else range(1, chips)
        return [gather_copy(k, h, source, row, d, row, same_core(d)) for d in reach] + [
            gather_copy(k, h, source, row, 0, row, partner)
        ]

    def passed_copy(k, h, d):
        slot = same_core(-d)
        return gather_copy(k, h, gathered.at[k, h, slot], slot, chips + d, slot, partner)

    def relay_copy(k, h, d):
        slot, which = same_core(d), pl.ds((d - 1) * (part // 2), part // 2)
        source = gathered.at[k, h, slot, which, :]
        recv = slot if d == 1 else n_row
        return gather_copy(k, h, source, slot, 3 if d == 1 else chips, recv, same_core(3 - d), which)

    def relay_arrival(k, h, d):
        slot, which = same_core(3), pl.ds((d - 1) * (part // 2), part // 2)
        place = gathered.at[k, h, slot, which, :]
        return gather_copy(k, h, place, slot, 0, slot if d == 1 else n_row, partner, which)

    def arrival(k, h, slot):
        return gather_copy(k, h, gathered.at[k, h, slot], slot, 0, slot, partner)

    def gather_start(k, h):
        for copy in own_copies(k, h):
            copy.start()

    def gather_pass(k, h):
        if relay:
            for d in range(1, 3):
                arrival(k, h, same_core(d)).wait_recv()
                relay_copy(k, h, d).start()
                passed_copy(k, h, d).start()

    def gather_finish(k, h):
        if relay:
            for d in range(1, 3):
                relay_arrival(k, h, d).wait_recv()
            passed_copy(k, h, 3).start()
        else:
            for d in range(1, chips):
                arrival(k, h, same_core(-d)).wait_recv()
                passed_copy(k, h, d).start()
        arrival(k, h, partner).wait_recv()
        for d in range(1, chips):
            arrival(k, h, other_core(-d)).wait_recv()

    def target_of(d):
        above, below = n_col - 1 - col, col
        lower = jnp.where(d < above, n_col - 1 - d, d - above)
        upper = jnp.where(d < below, d, n_col - 1 - (d - below))
        return jnp.where(2 * col < n_col, lower, upper)

    def share_copy(k, h, target):
        to = jnp.where(target > col, col + 1, col - 1)
        slot = jnp.where((target < col) & (to == target), n_col, target)
        return pltpu.make_async_remote_copy(
            src_ref=partial.at[k, h, target],
            dst_ref=landed.at[k, h, slot],
            send_sem=share_send.at[k, h, target],
            recv_sem=share_recv.at[k, h, slot],
            device_id=(row, to),
            device_id_type=MESH,
        )

    def share_arrival(k, h, slot):
        return pltpu.make_async_remote_copy(
            src_ref=partial.at[k, h, 0],
            dst_ref=landed.at[k, h, slot],
            send_sem=share_send.at[k, h, 0],
            recv_sem=share_recv.at[k, h, slot],
            device_id=(row, (col + 1) % n_col),
            device_id_type=MESH,
        )

    wide = min(piece_len, 4 * LANES)

    def add_landed(k, h, target, slot):
        def some(t, carry):
            at = pl.ds(pl.multiple_of(t * wide, wide), wide)
            partial[k, h, target, :, at] = partial[k, h, target, :, at] + landed[k, h, slot, :, at]
            return carry

        lax.fori_loop(0, piece_len // wide, some, 0)

    def at_the_end(target):
        return jnp.where(target > col, col == 0, col == n_col - 1)

    def forward(k, h, d):
        target = target_of(d)

        @pl.when(jnp.logical_not(at_the_end(target)))
        def _():
            share_arrival(k, h, target).wait_recv()
            add_landed(k, h, target, target)
            share_copy(k, h, target).start()

    def forward_some(k, h, first, last):
        def one(d, carry):
            forward(k, h, d)
            return carry

        lax.fori_loop(first, last, one, 0)

    chunk = raw.shape[2] * SUBLANES
    chunks = rows // chunk

    def fetch(index, slot):
        first = pl.multiple_of(index * (chunk // SUBLANES), chunk // SUBLANES)
        return [
            pltpu.make_async_copy(
                coupling_ref.at[s, pl.ds(first, chunk // SUBLANES), :, i, :],
                raw.at[slot, s, :, i],
                raw_sem.at[slot, s, i],
            )
            for s in range(slots)
            for i in range(SUBLANES)
        ]

    def prepare_chunk(index, carry):
        slot = index % 2

        @pl.when(index + 1 < chunks)
        def _():
            for copy in fetch(index + 1, 1 - slot):
                copy.start()

        for copy in fetch(index, slot):
            copy.wait()
        low = low_half((BLOCK // 2, LANES))

        def eight(j, carry):
            for i in range(SUBLANES):
                at = index * chunk + j * SUBLANES + i
                for q in range(pairs):
                    one = raw[slot, 2 * q, j, i]
                    one_turned = pltpu.roll(one, BLOCK, 1)
                    if 2 * q + 1 < slots:
                        two = raw[slot, 2 * q + 1, j, i]
                        two_turned = pltpu.roll(two, BLOCK, 1)
                    else:
                        two = two_turned = jnp.zeros_like(one)
                    both = jnp.concatenate([jnp.where(low, one, two_turned), jnp.where(low, one_turned, two)], axis=0)
                    high, rest = split(both)
                    prepared[at, :BLOCK, q * LANES : (q + 1) * LANES] = high
                    prepared[at, BLOCK:, q * LANES : (q + 1) * LANES] = rest
            return carry

        lax.fori_loop(0, chunk // SUBLANES, eight, 0)
        return carry

    def fill(k, h):
        low = low_half((part, LANES))

        def one(index, carry):
            for t in range(tiles):
                x = gathered[k, h, index, :, t * LANES : (t + 1) * LANES]
                turned = pltpu.roll(x, BLOCK, 1)
                for side, value in enumerate((jnp.where(low, x, turned), jnp.where(low, turned, x))):
                    high, rest = split(value)
                    place = index * (2 * tiles) + 2 * t + side
                    blocks[place, :part, :] = high
                    blocks[place, part:, :] = rest
            return carry

        lax.fori_loop(0, n_row, one, 0)

    def compute(k, h, first, last):
        low = low_half((part, LANES))
        low_picked = low_half((2 * part, LANES))

        def one_part(d, carry):
            target = target_of(d)

            def some_rows(step, carry):
                at = target * per_piece + step * group
                done = []
                for i in range(group):
                    base = (at + i) * slots
                    picked = [blocks[places_ref[base + s]] for s in range(slots)]
                    sides = [
                        jnp.where(low_picked, picked[2 * q], picked[2 * q + 1]) if 2 * q + 1 < slots else picked[2 * q]
                        for q in range(pairs)
                    ]
                    product = lax.dot_general(
                        jnp.concatenate(sides, axis=1),
                        prepared[at + i],
                        (((1,), (1,)), ((), ())),
                        preferred_element_type=jnp.float32,
                    )
                    total = product[:part] + product[part:]
                    done.append(total + pltpu.roll(total, BLOCK, 1))
                width = group * BLOCK
                joined = [jnp.where(low, done[2 * q], done[2 * q + 1]) for q in range(group // 2)]
                partial[k, h, target, :, pl.ds(pl.multiple_of(step * width, width), width)] = jnp.concatenate(joined, axis=1)
                return carry

            lax.fori_loop(0, per_piece // group, some_rows, 0)

            @pl.when((target != col) & at_the_end(target))
            def _():
                share_copy(k, h, target).start()

            return carry

        lax.fori_loop(first, last, one_part, 0)

    def update(k, h):
        @pl.when(col > 0)
        def _():
            share_arrival(k, h, col).wait_recv()
            add_landed(k, h, col, col)

        @pl.when(col < n_col - 1)
        def _():
            share_arrival(k, h, n_col).wait_recv()
            add_landed(k, h, col, n_col)

        here = slice(h * part, (h + 1) * part)
        lane = lax.broadcasted_iota(jnp.int32, (part, LANES), 1)
        order = lane // BLOCK * BLOCK + lane % 2 * (BLOCK // 2) + lane % BLOCK // 2

        def tile(t, carry):
            at = pl.ds(pl.multiple_of(t * LANES, LANES), LANES)
            total = jnp.take_along_axis(partial[k, h, col, :, at], order, axis=1)
            total = energies_ref[:, at] * terms[k][here, at] + total
            if k > 0:
                total = 2.0 * total - terms[k - 1][here, at]
            terms[k + 1][here, at] = total
            if k + 1 < DEGREE:
                gathered[k + 1, h, row, :, at] = total
            return carry

        lax.fori_loop(0, tiles, tile, 0)

    stages = [(k, h) for k in range(DEGREE) for h in range(halves)]
    early = n_col // 2
    soon = max(n_col - 3, 0)

    for copy in fetch(0, 0):
        copy.start()
    gather_start(0, 0)
    for h in range(halves):
        gathered[0, h, row] = share_of(0, h)[...]
    lax.fori_loop(0, chunks // 2, prepare_chunk, 0)
    gather_pass(0, 0)
    for h in range(1, halves):
        gather_start(0, h)
    lax.fori_loop(chunks // 2, chunks, prepare_chunk, 0)
    gather_finish(0, 0)
    fill(0, 0)

    for index, (k, h) in enumerate(stages):
        later = stages[index + 1] if index + 1 < len(stages) else None
        compute(k, h, 0, early)
        if index > 0:
            update(*stages[index - 1])
            if later is not None and later[0] > 0:
                gather_start(*later)
        compute(k, h, early, n_col - 1)
        forward_some(k, h, 0, soon)
        compute(k, h, n_col - 1, n_col)
        if later is not None:
            gather_pass(*later)
        forward_some(k, h, soon, n_col - 1)
        if later is not None:
            gather_finish(*later)
            fill(*later)
    update(*stages[-1])

    for k in range(DEGREE):
        for h in range(halves):
            for copy in own_copies(k, h) + [passed_copy(k, h, d) for d in range(1, chips)]:
                copy.wait_send()
            if relay:
                for d in range(1, 3):
                    relay_copy(k, h, d).wait_send()

            def one(d, carry):
                share_copy(k, h, target_of(d)).wait_send()
                return carry

            lax.fori_loop(0, n_col - 1, one, 0)


def shards(start_modes, energies, coupling, pattern):
    n_row, n_col = lax.axis_size("row"), lax.axis_size("col")
    modes, piece_len = start_modes.shape
    per_piece = piece_len // BLOCK
    rows, slots, entries = coupling.shape
    pairs = (slots + 1) // 2
    chunk, halves = 32, 2
    part = modes // halves
    tall = entries // LANES
    places = (pattern // per_piece // n_col * per_piece + pattern % per_piece).reshape(-1)
    by_slot = jnp.transpose(coupling, (1, 0, 2)).reshape(slots, rows // SUBLANES, SUBLANES, tall, LANES)
    vmem = pl.BlockSpec(memory_space=pltpu.VMEM)
    filtered, previous = pl.pallas_call(
        functools.partial(filter_kernel, slots, n_row, n_col, halves),
        in_specs=[pl.BlockSpec(memory_space=pltpu.SMEM), vmem, vmem, pl.BlockSpec(memory_space=pl.ANY)],
        out_specs=[vmem, vmem],
        out_shape=[jax.ShapeDtypeStruct(start_modes.shape, jnp.float32)] * 2,
        scratch_shapes=[
            pltpu.VMEM((2, slots, chunk // SUBLANES, SUBLANES, tall, LANES), jnp.float32),
            pltpu.VMEM((rows, 2 * BLOCK, pairs * LANES), jnp.bfloat16),
            pltpu.VMEM((DEGREE, halves, n_row, part, piece_len), jnp.float32),
            pltpu.VMEM((n_row * per_piece, 2 * part, LANES), jnp.bfloat16),
            pltpu.VMEM((modes, piece_len), jnp.float32),
            pltpu.VMEM((DEGREE, halves, n_col, part, piece_len), jnp.float32),
            pltpu.VMEM((DEGREE, halves, n_col + 1, part, piece_len), jnp.float32),
            pltpu.SemaphoreType.DMA((2, slots, SUBLANES)),
            pltpu.SemaphoreType.DMA((DEGREE, halves, n_row)),
            pltpu.SemaphoreType.DMA((DEGREE, halves, n_row + 1)),
            pltpu.SemaphoreType.DMA((DEGREE, halves, n_col)),
            pltpu.SemaphoreType.DMA((DEGREE, halves, n_col + 1)),
        ],
        compiler_params=pltpu.CompilerParams(collective_id=0, has_side_effects=True, vmem_limit_bytes=67043328),
        name="filter",
    )(places, start_modes, energies.reshape(1, -1), jnp.transpose(by_slot, (0, 1, 3, 2, 4)))
    return filtered, previous


def solution(mesh):
    in_specs = (P(None, ("row", "col")), P(("row", "col")), P("row", "col", None), P("row", "col"))
    out_specs = (P(None, ("row", "col")), P(None, ("row", "col")))
    return jax.shard_map(shards, mesh=mesh, in_specs=in_specs, out_specs=out_specs, check_vma=False)
```

time: 191 us -> 171 us (0.90)
  Pallas kernels: 185 us -> 164 us
    pallas_call x1, Pallas kernels: 185 us -> 164 us  [shards(): pl.pallas_call(functools.partial(filter_kernel, slots, n_row, n_col, halv...]
where the time goes in v1:
time: 171 us; the launch traced here: 170 us
  Pallas kernels  164 us (96%)
  local copies, waits for them, and re-layouts  4.68 us (3%)
    pallas_call x1, Pallas kernels, shards(): pl.pallas_call(functools.partial(filter_kernel, slots, n_row, n_col, halv...  164 us
    unnamed x2, local copies, waits for them, and re-layouts  3.74 us

profile of v1, /device:TPU:0, one launch (start us, length us, event | category | flops | bytes accessed | tf_op | source)
XLA Modules:
  0.0 170.2 jit_solution(13345137196721191985)
XLA Ops:
  0.6 0.7 fusion.2
  1.3 0.1 copy.6
  1.5 0.8 reshape.13.places_ref
  2.3 164.1 %filter.1 = (f32[32,4096]{1,0:T(8,128)}, f32[32,4096]{1,0:T(8,128)}) custom-call(s32[1280]{0:T(1024)} %reshape.13.places_ref, f32[32,4096]{1,0:T(8,128)} %start_ref.1, f32[1,4096]{1,0:T(1,128)} %bitcast.7, f32[5,32,32,8,128]{4,3,2,1,0:T(8,128)} %bitcast.6), custom_call_target="tpu_custom_call" | custom-call | tf_op jit(solution)/shard_map/filter/pallas_call | solution.py:385
  166.4 1.9 %copy.9 = f32[32,4096]{1,0:T(8,128)} copy(f32[32,4096]{1,0:T(8,128)} %get-tuple-element.4) | data formatting | bytes 1048576
  168.3 1.9 %copy.10 = f32[32,4096]{1,0:T(8,128)} copy(f32[32,4096]{1,0:T(8,128)} %get-tuple-element.5) | data formatting | bytes 1048576

commit v2 on v1

--- a/solution.py
+++ b/solution.py
@@ -112,25 +112,27 @@
         for copy in own_copies(k, h):
             copy.start()
 
+    near = range(1, 3) if relay else range(1, chips)
+
     def gather_pass(k, h):
-        if relay:
-            for d in range(1, 3):
-                arrival(k, h, same_core(d)).wait_recv()
+        for d in near:
+            arrival(k, h, same_core(-d)).wait_recv()
+            if relay:
                 relay_copy(k, h, d).start()
-                passed_copy(k, h, d).start()
+            passed_copy(k, h, d).start()
+        fill(k, h, [row] + [same_core(-d) for d in near])
 
     def gather_finish(k, h):
+        arrival(k, h, partner).wait_recv()
+        for d in near:
+            arrival(k, h, other_core(-d)).wait_recv()
+        fill(k, h, [partner] + [other_core(-d) for d in near])
         if relay:
             for d in range(1, 3):
                 relay_arrival(k, h, d).wait_recv()
             passed_copy(k, h, 3).start()
-        else:
-            for d in range(1, chips):
-                arrival(k, h, same_core(-d)).wait_recv()
-                passed_copy(k, h, d).start()
-        arrival(k, h, partner).wait_recv()
-        for d in range(1, chips):
-            arrival(k, h, other_core(-d)).wait_recv()
+            arrival(k, h, other_core(3)).wait_recv()
+            fill(k, h, [same_core(3), other_core(3)])
 
     def target_of(d):
         above, below = n_col - 1 - col, col
@@ -160,7 +162,7 @@
             device_id_type=MESH,
         )
 
-    wide = min(piece_len, 4 * LANES)
+    wide = min(piece_len, 8 * LANES)
 
     def add_landed(k, h, target, slot):
         def some(t, carry):
@@ -236,10 +238,13 @@
         lax.fori_loop(0, chunk // SUBLANES, eight, 0)
         return carry
 
-    def fill(k, h):
+    def fill(k, h, indices):
         low = low_half((part, LANES))
 
-        def one(index, carry):
+        def one(n, carry):
+            index = indices[0]
+            for m, other in enumerate(indices[1:], 1):
+                index = jnp.where(n == m, other, index)
             for t in range(tiles):
                 x = gathered[k, h, index, :, t * LANES : (t + 1) * LANES]
                 turned = pltpu.roll(x, BLOCK, 1)
@@ -250,7 +255,7 @@
                     blocks[place, part:, :] = rest
             return carry
 
-        lax.fori_loop(0, n_row, one, 0)
+        lax.fori_loop(0, len(indices), one, 0)
 
     def compute(k, h, first, last):
         low = low_half((part, LANES))
@@ -296,29 +301,29 @@
         @pl.when(col > 0)
         def _():
             share_arrival(k, h, col).wait_recv()
-            add_landed(k, h, col, col)
 
         @pl.when(col < n_col - 1)
         def _():
             share_arrival(k, h, n_col).wait_recv()
-            add_landed(k, h, col, n_col)
 
         here = slice(h * part, (h + 1) * part)
         lane = lax.broadcasted_iota(jnp.int32, (part, LANES), 1)
         order = lane // BLOCK * BLOCK + lane % 2 * (BLOCK // 2) + lane % BLOCK // 2
 
-        def tile(t, carry):
-            at = pl.ds(pl.multiple_of(t * LANES, LANES), LANES)
-            total = jnp.take_along_axis(partial[k, h, col, :, at], order, axis=1)
-            total = energies_ref[:, at] * terms[k][here, at] + total
-            if k > 0:
-                total = 2.0 * total - terms[k - 1][here, at]
-            terms[k + 1][here, at] = total
-            if k + 1 < DEGREE:
-                gathered[k + 1, h, row, :, at] = total
-            return carry
-
-        lax.fori_loop(0, tiles, tile, 0)
+        def some(t, carry):
+            for u in range(wide // LANES):
+                at = pl.ds(pl.multiple_of(t * wide + u * LANES, LANES), LANES)
+                total = partial[k, h, col, :, at] + landed[k, h, col, :, at] + landed[k, h, n_col, :, at]
+                total = jnp.take_along_axis(total, order, axis=1)
+                total = energies_ref[:, at] * terms[k][here, at] + total
+                if k > 0:
+                    total = 2.0 * total - terms[k - 1][here, at]
+                terms[k + 1][here, at] = total
+                if k + 1 < DEGREE:
+                    gathered[k + 1, h, row, :, at] = total
+            return carry
+
+        lax.fori_loop(0, piece_len // wide, some, 0)
 
     stages = [(k, h) for k in range(DEGREE) for h in range(halves)]
     early = n_col // 2
@@ -327,6 +332,15 @@
     for copy in fetch(0, 0):
         copy.start()
     gather_start(0, 0)
+
+    @pl.when(col == 0)
+    def _():
+        landed[:, :, 0, :, :] = jnp.zeros_like(landed[:, :, 0, :, :])
+
+    @pl.when(col == n_col - 1)
+    def _():
+        landed[:, :, n_col, :, :] = jnp.zeros_like(landed[:, :, n_col, :, :])
+
     for h in range(halves):
         gathered[0, h, row] = share_of(0, h)[...]
     lax.fori_loop(0, chunks // 2, prepare_chunk, 0)
@@ -335,7 +349,6 @@
         gather_start(0, h)
     lax.fori_loop(chunks // 2, chunks, prepare_chunk, 0)
     gather_finish(0, 0)
-    fill(0, 0)
 
     for index, (k, h) in enumerate(stages):
         later = stages[index + 1] if index + 1 < len(stages) else None
@@ -352,7 +365,6 @@
         forward_some(k, h, soon, n_col - 1)
         if later is not None:
             gather_finish(*later)
-            fill(*later)
     update(*stages[-1])
 
     for k in range(DEGREE):
@@ -368,6 +380,17 @@
                 return carry
 
             lax.fori_loop(0, n_col - 1, one, 0)
+
+
+def hand_over(filtered_ref, previous_ref, filtered_out, previous_out, sems):
+    copies = [
+        pltpu.make_async_copy(filtered_ref, filtered_out, sems.at[0]),
+        pltpu.make_async_copy(previous_ref, previous_out, sems.at[1]),
+    ]
+    for copy in copies:
+        copy.start()
+    for copy in copies:
+        copy.wait()
 
 
 def shards(start_modes, energies, coupling, pattern):
@@ -404,7 +427,15 @@
         compiler_params=pltpu.CompilerParams(collective_id=0, has_side_effects=True, vmem_limit_bytes=67043328),
         name="filter",
     )(places, start_modes, energies.reshape(1, -1), jnp.transpose(by_slot, (0, 1, 3, 2, 4)))
-    return filtered, previous
+    anywhere = pl.BlockSpec(memory_space=pl.ANY)
+    return pl.pallas_call(
+        hand_over,
+        in_specs=[vmem] * 2,
+        out_specs=[anywhere] * 2,
+        out_shape=[jax.ShapeDtypeStruct(start_modes.shape, jnp.float32)] * 2,
+        scratch_shapes=[pltpu.SemaphoreType.DMA((2,))],
+        name="hand_over",
+    )(filtered, previous)
 
 
 def solution(mesh):

time: 171 us -> 156 us (0.912)
  Pallas kernels: 164 us -> 153 us
  local copies, waits for them, and re-layouts: 4.68 us -> 0.94 us
    pallas_call x1, Pallas kernels: 164 us -> 150 us  [shards(): pl.pallas_call(functools.partial(filter_kernel, slots, n_row, n_col, halv...]
    unnamed x2 -> x0, local copies, waits for them, and re-layouts: 3.74 us -> none
    pallas_call x0 -> x1, Pallas kernels: none -> 2.18 us  [shards(): pl.pallas_call(hand_over, in_specs=[vmem] * 2, out_specs=[anywhere] * 2,...]
where the time goes in v2:
time: 156 us; the launch traced here: 155 us
  Pallas kernels  153 us (98%)
    pallas_call x1, Pallas kernels, shards(): pl.pallas_call(functools.partial(filter_kernel, slots, n_row, n_col, halv...  150 us

profile of v2, /device:TPU:0, one launch (start us, length us, event | category | flops | bytes accessed | tf_op | source)
XLA Modules:
  0.0 155.0 jit_solution(10552422675371200447)
XLA Ops:
  0.6 0.7 fusion.2
  1.3 0.1 copy.6
  1.5 0.8 reshape.13.places_ref
  2.3 150.5 %filter.1 = (f32[32,4096]{1,0:T(8,128)}, f32[32,4096]{1,0:T(8,128)}) custom-call(s32[1280]{0:T(1024)} %reshape.13.places_ref, f32[32,4096]{1,0:T(8,128)} %start_ref.1, f32[1,4096]{1,0:T(1,128)} %bitcast.7, f32[5,32,32,8,128]{4,3,2,1,0:T(8,128)} %bitcast.6), custom_call_target="tpu_custom_call" | custom-call | tf_op jit(solution)/shard_map/filter/pallas_call | solution.py:408
  152.8 2.2 %hand_over.1 = (f32[32,4096]{1,0:T(8,128)}, f32[32,4096]{1,0:T(8,128)}) custom-call(f32[32,4096]{1,0:T(8,128)} %get-tuple-element.4.filtered_ref, f32[32,4096]{1,0:T(8,128)} %get-tuple-element.5.previous_ref), custom_call_target="tpu_custom_call" | custom-call | tf_op jit(solution)/shard_map/hand_over/pallas_call | solution.py:431

commit v3 on v0

v3 whole, which is shorter than its diff:
```python
import functools

import jax
import jax.numpy as jnp
from jax import lax
from jax.experimental import pallas as pl
from jax.experimental.pallas import tpu as pltpu
from jax.sharding import PartitionSpec as P

BLOCK = 64
DEGREE = 3
LANES = 128
SUBLANES = 8


def low_half(shape):
    return lax.broadcasted_iota(jnp.int32, shape, len(shape) - 1) < BLOCK


def split(x):
    high = x.astype(jnp.bfloat16)
    return high, (x - high.astype(jnp.float32)).astype(jnp.bfloat16)


MESH = pl.DeviceIdType.MESH


def schedule(n_col):
    if n_col == 4:
        return (
            ("compute", 0, 2), ("update",), ("gather",), ("forward", 0, 1), ("compute", 2, 4), ("forward", 1, 2),
            ("compute", 4, 5), ("forward", 4, 5), ("relay",), ("forward", 2, 3), ("compute", 5, 6), ("pass",),
            ("fill near",), ("forward", 5, 6), ("forward", 3, 4), ("compute", 6, 7), ("fill other",), ("far",),
            ("compute", 7, 8), ("fill far",),
        )
    others = 2 * (n_col - 1)
    return (
        ("compute", 0, 2), ("update",), ("gather",), ("compute", 2, others), ("relay",), ("pass",), ("fill near",),
        ("forward", 0, others), ("compute", others, others + 2), ("fill other",), ("far",), ("fill far",),
    )


def filter_kernel(
    slots, n_row, n_col, halves,
    places_ref, start_ref, energies_ref, coupling_ref, filtered_ref, previous_ref,
    raw, prepared, gathered, blocks, terms, partial, landed,
    raw_sem, local_sem, gather_send, gather_recv, share_send, share_recv,
):
    row, col = lax.axis_index("row"), lax.axis_index("col")
    chips = n_row // 2
    chip, core = row // 2, row % 2
    partner = chip * 2 + (1 - core)
    part, side_len = terms.shape[3:]
    tiles = side_len // LANES
    per_side = side_len // BLOCK
    per_piece = 2 * per_side
    rows = prepared.shape[0]
    group = min(16, per_side)
    pairs = (slots + 1) // 2
    stages = DEGREE * halves
    relay = chips == 4
    wide = min(side_len, 8 * LANES)

    def other_chip(d):
        if chips & (chips - 1):
            return (chip + d) % chips
        place, bit, rest = chip, 1, abs(d)
        while rest:
            if rest % 2:
                place = place + bit * (1 - 2 * (chip // bit % 2))
            bit, rest = 2 * bit, rest // 2
        return place

    def same_core(d):
        return other_chip(d) * 2 + core

    def other_core(d):
        return other_chip(d) * 2 + (1 - core)

    def mode_copies(outward, ref, degree, h, sem):
        copies = []
        for side in range(2):
            near, far = terms.at[degree, h, side], ref.at[pl.ds(h * part, part), pl.ds(side * side_len, side_len)]
            source, place = (near, far) if outward else (far, near)
            copies.append(pltpu.make_async_copy(source, place, local_sem.at[sem, h, side]))
        return copies

    chunk = raw.shape[2] * SUBLANES
    chunks = rows // chunk

    def fetch(index, slot):
        first = pl.multiple_of(index * (chunk // SUBLANES), chunk // SUBLANES)
        return [
            pltpu.make_async_copy(
                coupling_ref.at[s, pl.ds(first, chunk // SUBLANES), :, i, :],
                raw.at[slot, s, :, i],
                raw_sem.at[slot, s, i],
            )
            for s in range(slots)
            for i in range(SUBLANES)
        ]

    for h in range(halves):
        for copy in mode_copies(False, start_ref, 0, h, 0):
            copy.start()
    for copy in fetch(0, 0):
        copy.start()

    barrier = pltpu.get_barrier_semaphore()
    for d in range(1, chips):
        pl.semaphore_signal(barrier, inc=1, device_id=(same_core(d), col), device_id_type=MESH)
    pl.semaphore_signal(barrier, inc=1, device_id=(partner, col), device_id_type=MESH)
    for d in (1, n_col - 1):
        pl.semaphore_signal(barrier, inc=1, device_id=(row, (col + d) % n_col), device_id_type=MESH)

    @pl.when(col == 0)
    def _():
        landed[:, 0] = jnp.zeros_like(landed[:, 0])

    @pl.when(col == n_col - 1)
    def _():
        landed[:, n_col] = jnp.zeros_like(landed[:, n_col])

    for h in range(halves):
        for copy in mode_copies(False, start_ref, 0, h, 0):
            copy.wait()
        gathered[h, row] = terms[0, h]
    pl.semaphore_wait(barrier, chips + 2)

    def gather_copy(stage, slot, side, send, target):
        place = gathered.at[stage, slot] if side is None else gathered.at[stage, slot, side]
        return pltpu.make_async_remote_copy(
            src_ref=place,
            dst_ref=place,
            send_sem=gather_send.at[stage, send],
            recv_sem=gather_recv.at[stage, 2 * slot + (side or 0)],
            device_id=(target, col),
            device_id_type=MESH,
        )

    def own_copies(stage):
        if not relay:
            return [gather_copy(stage, row, None, d, same_core(d)) for d in range(1, chips)] + [
                gather_copy(stage, row, None, 0, partner)
            ]
        return [
            gather_copy(stage, row, 0, 0, same_core(1)),
            gather_copy(stage, row, 1, 2, same_core(2)),
            gather_copy(stage, row, 1, 1, same_core(1)),
            gather_copy(stage, row, 0, 3, same_core(2)),
            gather_copy(stage, row, None, 4, partner),
        ]

    def relay_copies(stage):
        return [
            gather_copy(stage, same_core(1), 0, 5, same_core(2)),
            gather_copy(stage, same_core(2), 1, 6, same_core(1)),
        ]

    def passed_copy(stage, d):
        return gather_copy(stage, same_core(-d), None, (6 if relay else chips) + d, partner)

    def arrival(stage, slot, side=None):
        return gather_copy(stage, slot, side, 0, partner)

    def fill(stage, indices):
        low = low_half((part, LANES))
        h = stage % halves

        def one(m, carry):
            n, side = m // 2, m % 2
            index = indices[0]
            for other, value in enumerate(indices[1:], 1):
                index = jnp.where(n == other, value, index)
            for t in range(tiles):
                x = gathered[stage, index, side, :, t * LANES : (t + 1) * LANES]
                turned = pltpu.roll(x, BLOCK, 1)
                for half, value in enumerate((jnp.where(low, x, turned), jnp.where(low, turned, x))):
                    high, rest = split(value)
                    place = index * per_piece + side * per_side + 2 * t + half
                    blocks[h, place, :part, :] = high
                    blocks[h, place, part:, :] = rest
            return carry

        lax.fori_loop(0, 2 * len(indices), one, 0)

    near = range(1, 3) if relay else range(1, chips)

    def gather_step(step, stage):
        if step == "gather":
            for copy in own_copies(stage):
                copy.start()
        elif step == "relay":
            if relay:
                for (d, side), copy in zip(((1, 0), (2, 1)), relay_copies(stage)):
                    arrival(stage, same_core(d), side).wait_recv()
                    copy.start()
        elif step == "pass":
            for d in near:
                arrival(stage, same_core(-d), 2 - d if relay else None).wait_recv()
                passed_copy(stage, d).start()
        elif step == "fill near":
            fill(stage, [row] + [same_core(-d) for d in near])
        elif step == "fill other":
            arrival(stage, partner).wait_recv()
            for d in near:
                arrival(stage, other_core(-d)).wait_recv()
            fill(stage, [partner] + [other_core(-d) for d in near])
        elif step == "far":
            if relay:
                for side in range(2):
                    arrival(stage, same_core(3), side).wait_recv()
                passed_copy(stage, 3).start()
                fill(stage, [same_core(3)])
        elif step == "fill far":
            if relay:
                arrival(stage, other_core(3)).wait_recv()
                fill(stage, [other_core(3)])

    def target_of(d):
        above, below = n_col - 1 - col, col
        lower = jnp.where(d < above, n_col - 1 - d, d - above)
        upper = jnp.where(d < below, d, n_col - 1 - (d - below))
        return jnp.where(2 * col < n_col, lower, upper)

    def share_copy(stage, target, side):
        to = jnp.where(target > col, col + 1, col - 1)
        slot = jnp.where((target < col) & (to == target), n_col, target)
        return pltpu.make_async_remote_copy(
            src_ref=partial.at[stage, target, side],
            dst_ref=landed.at[stage, slot, side],
            send_sem=share_send.at[stage, 2 * target + side],
            recv_sem=share_recv.at[stage, 2 * slot + side],
            device_id=(row, to),
            device_id_type=MESH,
        )

    def share_arrival(stage, slot, side):
        return pltpu.make_async_remote_copy(
            src_ref=partial.at[stage, 0, side],
            dst_ref=landed.at[stage, slot, side],
            send_sem=share_send.at[stage, side],
            recv_sem=share_recv.at[stage, 2 * slot + side],
            device_id=(row, (col + 1) % n_col),
            device_id_type=MESH,
        )

    def at_the_end(target):
        return jnp.where(target > col, col == 0, col == n_col - 1)

    def forward(stage, first, last):
        def one(j, carry):
            target, side = target_of(j // 2), j % 2

            @pl.when(jnp.logical_not(at_the_end(target)))
            def _():
                share_arrival(stage, target, side).wait_recv()

                def some(t, carry):
                    at = pl.ds(pl.multiple_of(t * wide, wide), wide)
                    partial[stage, target, side, :, at] = partial[stage, target, side, :, at] + landed[stage, target, side, :, at]
                    return carry

                lax.fori_loop(0, side_len // wide, some, 0)
                share_copy(stage, target, side).start()

            return carry

        lax.fori_loop(first, last, one, 0)

    def compute(stage, first, last):
        low = low_half((part, LANES))
        low_picked = low_half((2 * part, LANES))
        h = stage % halves

        def one(j, carry):
            target, side = target_of(j // 2), j % 2

            def some_rows(step, carry):
                at = target * per_piece + side * per_side + step * group
                done = []
                for i in range(group):
                    base = (at + i) * slots
                    picked = [blocks[h, places_ref[base + s]] for s in range(slots)]
                    sides = [
                        jnp.where(low_picked, picked[2 * q], picked[2 * q + 1]) if 2 * q + 1 < slots else picked[2 * q]
                        for q in range(pairs)
                    ]
                    product = lax.dot_general(
                        jnp.concatenate(sides, axis=1),
                        prepared[at + i],
                        (((1,), (1,)), ((), ())),
                        preferred_element_type=jnp.float32,
                    )
                    total = product[:part] + product[part:]
                    done.append(total + pltpu.roll(total, BLOCK, 1))
                width = group * BLOCK
                joined = [jnp.where(low, done[2 * q], done[2 * q + 1]) for q in range(group // 2)]
                there = pl.ds(pl.multiple_of(step * width, width), width)
                partial[stage, target, side, :, there] = jnp.concatenate(joined, axis=1)
                return carry

            lax.fori_loop(0, per_side // group, some_rows, 0)

            @pl.when((target != col) & at_the_end(target))
            def _():
                share_copy(stage, target, side).start()

            return carry

        lax.fori_loop(first, last, one, 0)

    def update(stage):
        k, h = stage // halves, stage % halves
        lane = lax.broadcasted_iota(jnp.int32, (part, LANES), 1)
        order = lane // BLOCK * BLOCK + lane % 2 * (BLOCK // 2) + lane % BLOCK // 2
        more = stage + halves < stages
        follower = jnp.minimum(stage + halves, stages - 1)
        before = jnp.maximum(k - 1, 0)
        for side in range(2):

            @pl.when(col > 0)
            def _():
                share_arrival(stage, col, side).wait_recv()

            @pl.when(col < n_col - 1)
            def _():
                share_arrival(stage, n_col, side).wait_recv()

            def some(t, carry):
                for u in range(wide // LANES):
                    at = pl.ds(pl.multiple_of(t * wide + u * LANES, LANES), LANES)
                    total = partial[stage, col, side, :, at] + landed[stage, col, side, :, at] + landed[stage, n_col, side, :, at]
                    total = jnp.take_along_axis(total, order, axis=1)
                    total = energies_ref[side, :, at] * terms[k, h, side, :, at] + total
                    total = jnp.where(k > 0, 2.0 * total - terms[before, h, side, :, at], total)
                    terms[k + 1, h, side, :, at] = total
                return carry

            lax.fori_loop(0, side_len // wide, some, 0)

        @pl.when(more)
        def _():
            gathered[follower, row] = terms[k + 1, h]

    def prepare_chunk(index, carry):
        slot = index % 2

        @pl.when(index + 1 < chunks)
        def _():
            for copy in fetch(index + 1, 1 - slot):
                copy.start()

        for copy in fetch(index, slot):
            copy.wait()
        low = low_half((BLOCK // 2, LANES))

        def eight(j, carry):
            for i in range(SUBLANES):
                at = index * chunk + j * SUBLANES + i
                for q in range(pairs):
                    one = raw[slot, 2 * q, j, i]
                    one_turned = pltpu.roll(one, BLOCK, 1)
                    if 2 * q + 1 < slots:
                        two = raw[slot, 2 * q + 1, j, i]
                        two_turned = pltpu.roll(two, BLOCK, 1)
                    else:
                        two = two_turned = jnp.zeros_like(one)
                    both = jnp.concatenate([jnp.where(low, one, two_turned), jnp.where(low, one_turned, two)], axis=0)
                    high, rest = split(both)
                    prepared[at, :BLOCK, q * LANES : (q + 1) * LANES] = high
                    prepared[at, BLOCK:, q * LANES : (q + 1) * LANES] = rest
            return carry

        lax.fori_loop(0, chunk // SUBLANES, eight, 0)
        return carry

    gather_step("gather", 0)
    lax.fori_loop(0, chunks // 4, prepare_chunk, 0)
    gather_step("relay", 0)
    lax.fori_loop(chunks // 4, chunks // 2, prepare_chunk, 0)
    gather_step("pass", 0)
    gather_step("fill near", 0)
    gather_step("gather", 1)
    lax.fori_loop(chunks // 2, chunks, prepare_chunk, 0)
    for step in ("fill other", "far", "fill far"):
        gather_step(step, 0)

    def one_stage(stage, carry):
        for step, *span in schedule(n_col):
            if step == "compute":
                compute(stage, *span)
            elif step == "forward":
                forward(stage, *span)
            elif step == "update":

                @pl.when(stage > 0)
                def _():
                    update(stage - 1)

            elif step == "gather":

                @pl.when((stage > 0) & (stage + 1 < stages))
                def _():
                    gather_step(step, stage + 1)

            else:

                @pl.when(stage + 1 < stages)
                def _():
                    gather_step(step, stage + 1)

        return carry

    lax.fori_loop(0, stages, one_stage, 0)
    update(stages - 1)
    outward = [(previous_ref, DEGREE - 1, 1), (filtered_ref, DEGREE, 2)]
    for ref, degree, sem in outward:
        for h in range(halves):
            for copy in mode_copies(True, ref, degree, h, sem):
                copy.start()

    def drain(stage, carry):
        for copy in own_copies(stage) + [passed_copy(stage, d) for d in range(1, chips)] + (relay_copies(stage) if relay else []):
            copy.wait_send()

        def one(j, carry):
            share_copy(stage, target_of(j // 2), j % 2).wait_send()
            return carry

        lax.fori_loop(0, 2 * (n_col - 1), one, 0)
        return carry

    lax.fori_loop(0, stages, drain, 0)
    for ref, degree, sem in outward:
        for h in range(halves):
            for copy in mode_copies(True, ref, degree, h, sem):
                copy.wait()


def hand_over(filtered_ref, previous_ref, filtered_out, previous_out, sems):
    copies = [
        pltpu.make_async_copy(filtered_ref, filtered_out, sems.at[0]),
        pltpu.make_async_copy(previous_ref, previous_out, sems.at[1]),
    ]
    for copy in copies:
        copy.start()
    for copy in copies:
        copy.wait()


def shards(start_modes, energies, coupling, pattern):
    n_row, n_col = lax.axis_size("row"), lax.axis_size("col")
    modes, piece_len = start_modes.shape
    per_piece = piece_len // BLOCK
    rows, slots, entries = coupling.shape
    pairs = (slots + 1) // 2
    chunk, halves = 16, 2
    part, side_len = modes // halves, piece_len // 2
    stages = DEGREE * halves
    tall = entries // LANES
    places = (pattern // per_piece // n_col * per_piece + pattern % per_piece).reshape(-1)
    by_slot = jnp.transpose(coupling, (1, 0, 2)).reshape(slots, rows // SUBLANES, SUBLANES, tall, LANES)
    vmem = pl.BlockSpec(memory_space=pltpu.VMEM)
    anywhere = pl.BlockSpec(memory_space=pl.ANY)
    filtered, previous = pl.pallas_call(
        functools.partial(filter_kernel, slots, n_row, n_col, halves),
        in_specs=[pl.BlockSpec(memory_space=pltpu.SMEM), anywhere, vmem, anywhere],
        out_specs=[anywhere, anywhere],
        out_shape=[jax.ShapeDtypeStruct(start_modes.shape, jnp.float32)] * 2,
        scratch_shapes=[
            pltpu.VMEM((2, slots, chunk // SUBLANES, SUBLANES, tall, LANES), jnp.float32),
            pltpu.VMEM((rows, 2 * BLOCK, pairs * LANES), jnp.bfloat16),
            pltpu.VMEM((stages, n_row, 2, part, side_len), jnp.float32),
            pltpu.VMEM((halves, n_row * per_piece, 2 * part, LANES), jnp.bfloat16),
            pltpu.VMEM((DEGREE + 1, halves, 2, part, side_len), jnp.float32),
            pltpu.VMEM((stages, n_col, 2, part, side_len), jnp.float32),
            pltpu.VMEM((stages, n_col + 1, 2, part, side_len), jnp.float32),
            pltpu.SemaphoreType.DMA((2, slots, SUBLANES)),
            pltpu.SemaphoreType.DMA((3, halves, 2)),
            pltpu.SemaphoreType.DMA((stages, max(10, n_row))),
            pltpu.SemaphoreType.DMA((stages, 2 * n_row)),
            pltpu.SemaphoreType.DMA((stages, 2 * n_col)),
            pltpu.SemaphoreType.DMA((stages, 2 * (n_col + 1))),
        ],
        compiler_params=pltpu.CompilerParams(collective_id=0, has_side_effects=True, vmem_limit_bytes=67043328),
        name="filter",
    )(places, start_modes, energies.reshape(2, 1, side_len), jnp.transpose(by_slot, (0, 1, 3, 2, 4)))
    return pl.pallas_call(
        hand_over,
        in_specs=[vmem] * 2,
        out_specs=[anywhere] * 2,
        out_shape=[jax.ShapeDtypeStruct(start_modes.shape, jnp.float32)] * 2,
        scratch_shapes=[pltpu.SemaphoreType.DMA((2,))],
        name="hand_over",
    )(filtered, previous)


def solution(mesh):
    in_specs = (P(None, ("row", "col")), P(("row", "col")), P("row", "col", None), P("row", "col"))
    out_specs = (P(None, ("row", "col")), P(None, ("row", "col")))
    return jax.shard_map(shards, mesh=mesh, in_specs=in_specs, out_specs=out_specs, check_vma=False)
```

time: 191 us -> 138 us (0.72)
  Pallas kernels: 185 us -> 134 us
  local copies, waits for them, and re-layouts: 4.68 us -> 0.94 us
    pallas_call x1, Pallas kernels: 185 us -> 132 us  [shards(): pl.pallas_call(functools.partial(filter_kernel, slots, n_row, n_col, halv...]
    unnamed x2 -> x0, local copies, waits for them, and re-layouts: 3.74 us -> none
    pallas_call x0 -> x1, Pallas kernels: none -> 2.18 us  [shards(): pl.pallas_call(hand_over, in_specs=[vmem] * 2, out_specs=[anywhere] * 2,...]
where the time goes in v3:
time: 138 us; the launch traced here: 136 us
  Pallas kernels  134 us (97%)
    pallas_call x1, Pallas kernels, shards(): pl.pallas_call(functools.partial(filter_kernel, slots, n_row, n_col, halv...  132 us

profile of v3, /device:TPU:0, one launch (start us, length us, event | category | flops | bytes accessed | tf_op | source)
XLA Modules:
  0.0 136.3 jit_solution(6578713108789942723)
XLA Ops:
  0.6 0.7 fusion.2
  1.3 0.1 copy.6
  1.5 0.8 reshape.13.places_ref
  2.3 131.8 %filter.1 = (f32[32,4096]{1,0:T(8,128)}, f32[32,4096]{1,0:T(8,128)}) custom-call(s32[1280]{0:T(1024)} %reshape.13.places_ref, f32[32,4096]{1,0:T(8,128)} %start_ref.1, f32[2,1,2048]{2,1,0:T(1,128)} %bitcast.7, f32[5,32,32,8,128]{4,3,2,1,0:T(8,128)} %bitcast.6), custom_call_target="tpu_custom_call" | custom-call | tf_op jit(solution)/shard_map/filter/pallas_call | solution.py:466
  134.1 2.2 %hand_over.1 = (f32[32,4096]{1,0:T(8,128)}, f32[32,4096]{1,0:T(8,128)}) custom-call(f32[32,4096]{1,0:T(8,128)} %get-tuple-element.4.filtered_ref, f32[32,4096]{1,0:T(8,128)} %get-tuple-element.5.previous_ref), custom_call_target="tpu_custom_call" | custom-call | tf_op jit(solution)/shard_map/hand_over/pallas_call | solution.py:489

commit v4 on v3

--- a/solution.py
+++ b/solution.py
@@ -30,19 +30,19 @@
         return (
             ("compute", 0, 2), ("update",), ("gather",), ("forward", 0, 1), ("compute", 2, 4), ("forward", 1, 2),
             ("compute", 4, 5), ("forward", 4, 5), ("relay",), ("forward", 2, 3), ("compute", 5, 6), ("pass",),
-            ("fill near",), ("forward", 5, 6), ("forward", 3, 4), ("compute", 6, 7), ("fill other",), ("far",),
-            ("compute", 7, 8), ("fill far",),
+            ("fill near",), ("forward", 5, 6), ("forward", 3, 4), ("prepare",), ("compute", 6, 7), ("fill other",),
+            ("far",), ("compute", 7, 8), ("drain",), ("fill far",),
         )
     others = 2 * (n_col - 1)
     return (
-        ("compute", 0, 2), ("update",), ("gather",), ("compute", 2, others), ("relay",), ("pass",), ("fill near",),
-        ("forward", 0, others), ("compute", others, others + 2), ("fill other",), ("far",), ("fill far",),
+        ("compute", 0, 2), ("update",), ("gather",), ("prepare",), ("compute", 2, others), ("relay",), ("pass",), ("fill near",),
+        ("forward", 0, others), ("compute", others, others + 2), ("fill other",), ("far",), ("drain",), ("fill far",),
     )
 
 
 def filter_kernel(
     slots, n_row, n_col, halves,
-    places_ref, start_ref, energies_ref, coupling_ref, filtered_ref, previous_ref,
+    pattern_ref, start_ref, energies_ref, coupling_ref, filtered_ref, previous_ref,
     raw, prepared, gathered, blocks, terms, partial, landed,
     raw_sem, local_sem, gather_send, gather_recv, share_send, share_recv,
 ):
@@ -85,11 +85,21 @@
             copies.append(pltpu.make_async_copy(source, place, local_sem.at[sem, h, side]))
         return copies
 
+    def target_of(d):
+        above, below = n_col - 1 - col, col
+        lower = jnp.where(d < above, n_col - 1 - d, d - above)
+        upper = jnp.where(d < below, d, n_col - 1 - (d - below))
+        return jnp.where(2 * col < n_col, lower, upper)
+
     chunk = raw.shape[2] * SUBLANES
     chunks = rows // chunk
 
+    def first_row(index):
+        per = per_piece // chunk
+        return target_of(index // per) * per_piece + index % per * chunk
+
     def fetch(index, slot):
-        first = pl.multiple_of(index * (chunk // SUBLANES), chunk // SUBLANES)
+        first = first_row(index) // SUBLANES
         return [
             pltpu.make_async_copy(
                 coupling_ref.at[s, pl.ds(first, chunk // SUBLANES), :, i, :],
@@ -217,12 +227,6 @@
                 arrival(stage, other_core(3)).wait_recv()
                 fill(stage, [other_core(3)])
 
-    def target_of(d):
-        above, below = n_col - 1 - col, col
-        lower = jnp.where(d < above, n_col - 1 - d, d - above)
-        upper = jnp.where(d < below, d, n_col - 1 - (d - below))
-        return jnp.where(2 * col < n_col, lower, upper)
-
     def share_copy(stage, target, side):
         to = jnp.where(target > col, col + 1, col - 1)
         slot = jnp.where((target < col) & (to == target), n_col, target)
@@ -268,6 +272,13 @@
 
         lax.fori_loop(first, last, one, 0)
 
+    def place_of(block):
+        if per_piece & (per_piece - 1) or n_col & (n_col - 1):
+            return block // per_piece // n_col * per_piece + block % per_piece
+        bits = per_piece.bit_length() - 1
+        piece = lax.shift_right_logical(block, bits + n_col.bit_length() - 1)
+        return lax.shift_left(piece, bits) + (block & (per_piece - 1))
+
     def compute(stage, first, last):
         low = low_half((part, LANES))
         low_picked = low_half((2 * part, LANES))
@@ -280,8 +291,7 @@
                 at = target * per_piece + side * per_side + step * group
                 done = []
                 for i in range(group):
-                    base = (at + i) * slots
-                    picked = [blocks[h, places_ref[base + s]] for s in range(slots)]
+                    picked = [blocks[h, place_of(pattern_ref[s, at + i])] for s in range(slots)]
                     sides = [
                         jnp.where(low_picked, picked[2 * q], picked[2 * q + 1]) if 2 * q + 1 < slots else picked[2 * q]
                         for q in range(pairs)
@@ -354,10 +364,11 @@
         for copy in fetch(index, slot):
             copy.wait()
         low = low_half((BLOCK // 2, LANES))
+        base = first_row(index)
 
         def eight(j, carry):
             for i in range(SUBLANES):
-                at = index * chunk + j * SUBLANES + i
+                at = base + j * SUBLANES + i
                 for q in range(pairs):
                     one = raw[slot, 2 * q, j, i]
                     one_turned = pltpu.roll(one, BLOCK, 1)
@@ -375,16 +386,32 @@
         lax.fori_loop(0, chunk // SUBLANES, eight, 0)
         return carry
 
+    def prepare(first, last):
+        lax.fori_loop(chunks * first // 16, chunks * last // 16, prepare_chunk, 0)
+
     gather_step("gather", 0)
-    lax.fori_loop(0, chunks // 4, prepare_chunk, 0)
+    prepare(0, 5)
     gather_step("relay", 0)
-    lax.fori_loop(chunks // 4, chunks // 2, prepare_chunk, 0)
+    prepare(5, 9)
     gather_step("pass", 0)
     gather_step("fill near", 0)
     gather_step("gather", 1)
-    lax.fori_loop(chunks // 2, chunks, prepare_chunk, 0)
-    for step in ("fill other", "far", "fill far"):
-        gather_step(step, 0)
+    prepare(9, 12)
+    gather_step("fill other", 0)
+    gather_step("far", 0)
+    prepare(12, 14)
+    gather_step("fill far", 0)
+
+    def drain_gather(stage):
+        for copy in own_copies(stage) + [passed_copy(stage, d) for d in range(1, chips)] + (relay_copies(stage) if relay else []):
+            copy.wait_send()
+
+    def drain_shares(stage):
+        def one(j, carry):
+            share_copy(stage, target_of(j // 2), j % 2).wait_send()
+            return carry
+
+        lax.fori_loop(0, 2 * (n_col - 1), one, 0)
 
     def one_stage(stage, carry):
         for step, *span in schedule(n_col):
@@ -392,6 +419,19 @@
                 compute(stage, *span)
             elif step == "forward":
                 forward(stage, *span)
+            elif step == "prepare":
+
+                @pl.when(stage == 0)
+                def _():
+                    prepare(14, 16)
+
+            elif step == "drain":
+                drain_gather(stage)
+
+                @pl.when(stage > 0)
+                def _():
+                    drain_shares(stage - 1)
+
             elif step == "update":
 
                 @pl.when(stage > 0)
@@ -420,32 +460,32 @@
             for copy in mode_copies(True, ref, degree, h, sem):
                 copy.start()
 
-    def drain(stage, carry):
-        for copy in own_copies(stage) + [passed_copy(stage, d) for d in range(1, chips)] + (relay_copies(stage) if relay else []):
-            copy.wait_send()
-
-        def one(j, carry):
-            share_copy(stage, target_of(j // 2), j % 2).wait_send()
-            return carry
-
-        lax.fori_loop(0, 2 * (n_col - 1), one, 0)
-        return carry
-
-    lax.fori_loop(0, stages, drain, 0)
+    drain_shares(stages - 1)
     for ref, degree, sem in outward:
         for h in range(halves):
             for copy in mode_copies(True, ref, degree, h, sem):
                 copy.wait()
 
 
-def hand_over(filtered_ref, previous_ref, filtered_out, previous_out, sems):
-    copies = [
-        pltpu.make_async_copy(filtered_ref, filtered_out, sems.at[0]),
-        pltpu.make_async_copy(previous_ref, previous_out, sems.at[1]),
-    ]
-    for copy in copies:
+def hand_over(filtered_ref, previous_ref, filtered_out, previous_out, held, sems):
+    pieces = held.shape[1]
+    tall = held.shape[2]
+
+    def copies(inward):
+        both = []
+        for a, (ref, out) in enumerate(((filtered_ref, filtered_out), (previous_ref, previous_out))):
+            for p in range(pieces):
+                there, here = (ref if inward else out).at[pl.ds(p * tall, tall), :], held.at[a, p]
+                source, place = (there, here) if inward else (here, there)
+                both.append(pltpu.make_async_copy(source, place, sems.at[0 if inward else 1, a, p]))
+        return both
+
+    for copy in copies(True):
         copy.start()
-    for copy in copies:
+    for came, goes in zip(copies(True), copies(False)):
+        came.wait()
+        goes.start()
+    for copy in copies(False):
         copy.wait()
 
 
@@ -455,11 +495,10 @@
     per_piece = piece_len // BLOCK
     rows, slots, entries = coupling.shape
     pairs = (slots + 1) // 2
-    chunk, halves = 16, 2
+    chunk, halves = min(16, per_piece), 2
     part, side_len = modes // halves, piece_len // 2
     stages = DEGREE * halves
     tall = entries // LANES
-    places = (pattern // per_piece // n_col * per_piece + pattern % per_piece).reshape(-1)
     by_slot = jnp.transpose(coupling, (1, 0, 2)).reshape(slots, rows // SUBLANES, SUBLANES, tall, LANES)
     vmem = pl.BlockSpec(memory_space=pltpu.VMEM)
     anywhere = pl.BlockSpec(memory_space=pl.ANY)
@@ -485,13 +524,13 @@
         ],
         compiler_params=pltpu.CompilerParams(collective_id=0, has_side_effects=True, vmem_limit_bytes=67043328),
         name="filter",
-    )(places, start_modes, energies.reshape(2, 1, side_len), jnp.transpose(by_slot, (0, 1, 3, 2, 4)))
+    )(pattern.T, start_modes, energies.reshape(2, 1, side_len), jnp.transpose(by_slot, (0, 1, 3, 2, 4)))
     return pl.pallas_call(
         hand_over,
-        in_specs=[vmem] * 2,
+        in_specs=[anywhere] * 2,
         out_specs=[anywhere] * 2,
         out_shape=[jax.ShapeDtypeStruct(start_modes.shape, jnp.float32)] * 2,
-        scratch_shapes=[pltpu.SemaphoreType.DMA((2,))],
+        scratch_shapes=[pltpu.VMEM((2, modes // SUBLANES, SUBLANES, piece_len), jnp.float32), pltpu.SemaphoreType.DMA((2, 2, modes // SUBLANES))],
         name="hand_over",
     )(filtered, previous)
 

time: 138 us -> 134 us (0.971)
  Pallas kernels: 134 us -> 132 us
    pallas_call x1, Pallas kernels: 132 us -> 130 us  [shards(): pl.pallas_call(functools.partial(filter_kernel, slots, n_row, n_col, halv...]
where the time goes in v4:
time: 134 us; the launch traced here: 133 us
  Pallas kernels  132 us (99%)
    pallas_call x1, Pallas kernels, shards(): pl.pallas_call(functools.partial(filter_kernel, slots, n_row, n_col, halv...  130 us

profile of v4, /device:TPU:0, one launch (start us, length us, event | category | flops | bytes accessed | tf_op | source)
XLA Modules:
  0.0 132.6 jit_solution(16329666674171538297)
XLA Ops:
  0.6 129.9 %filter.1 = (f32[32,4096]{1,0:T(8,128)}, f32[32,4096]{1,0:T(8,128)}) custom-call(s32[5,256]{1,0:T(8,128)} %bitcast.9, f32[32,4096]{1,0:T(8,128)} %start_ref.1, f32[2,1,2048]{2,1,0:T(1,128)} %bitcast.8, f32[5,32,32,8,128]{4,3,2,1,0:T(8,128)} %bitcast.7), custom_call_target="tpu_custom_call" | custom-call | tf_op jit(solution)/shard_map/filter/pallas_call | solution.py:505
  130.6 2.1 %hand_over.1 = (f32[32,4096]{1,0:T(8,128)}, f32[32,4096]{1,0:T(8,128)}) custom-call(f32[32,4096]{1,0:T(8,128)} %get-tuple-element.4.filtered_ref, f32[32,4096]{1,0:T(8,128)} %get-tuple-element.5.previous_ref), custom_call_target="tpu_custom_call" | custom-call | tf_op jit(solution)/shard_map/hand_over/pallas_call | solution.py:528

commit v5 on v4

--- a/solution.py
+++ b/solution.py
@@ -59,6 +59,7 @@
     pairs = (slots + 1) // 2
     stages = DEGREE * halves
     relay = chips == 4
+    near = range(1, 3) if relay else range(1, chips)
     wide = min(side_len, 8 * LANES)
 
     def other_chip(d):
@@ -77,13 +78,13 @@
     def other_core(d):
         return other_chip(d) * 2 + (1 - core)
 
-    def mode_copies(outward, ref, degree, h, sem):
-        copies = []
-        for side in range(2):
-            near, far = terms.at[degree, h, side], ref.at[pl.ds(h * part, part), pl.ds(side * side_len, side_len)]
-            source, place = (near, far) if outward else (far, near)
-            copies.append(pltpu.make_async_copy(source, place, local_sem.at[sem, h, side]))
-        return copies
+    def mode_copies(h):
+        return [
+            pltpu.make_async_copy(
+                start_ref.at[pl.ds(h * part, part), pl.ds(side * side_len, side_len)], terms.at[0, h, side], local_sem.at[h, side]
+            )
+            for side in range(2)
+        ]
 
     def target_of(d):
         above, below = n_col - 1 - col, col
@@ -91,7 +92,7 @@
         upper = jnp.where(d < below, d, n_col - 1 - (d - below))
         return jnp.where(2 * col < n_col, lower, upper)
 
-    chunk = raw.shape[2] * SUBLANES
+    ahead, chunk = raw.shape[0], raw.shape[2] * SUBLANES
     chunks = rows // chunk
 
     def first_row(index):
@@ -102,26 +103,33 @@
         first = first_row(index) // SUBLANES
         return [
             pltpu.make_async_copy(
-                coupling_ref.at[s, pl.ds(first, chunk // SUBLANES), :, i, :],
-                raw.at[slot, s, :, i],
-                raw_sem.at[slot, s, i],
+                coupling_ref.at[:, pl.ds(first, chunk // SUBLANES), :, i, :],
+                raw.at[slot, :, :, i],
+                raw_sem.at[slot, i],
             )
-            for s in range(slots)
             for i in range(SUBLANES)
         ]
 
     for h in range(halves):
-        for copy in mode_copies(False, start_ref, 0, h, 0):
+        for copy in mode_copies(h):
             copy.start()
-    for copy in fetch(0, 0):
-        copy.start()
+    for index in range(ahead - 1):
+        for copy in fetch(index, index):
+            copy.start()
 
     barrier = pltpu.get_barrier_semaphore()
-    for d in range(1, chips):
+    for d in near:
         pl.semaphore_signal(barrier, inc=1, device_id=(same_core(d), col), device_id_type=MESH)
     pl.semaphore_signal(barrier, inc=1, device_id=(partner, col), device_id_type=MESH)
-    for d in (1, n_col - 1):
-        pl.semaphore_signal(barrier, inc=1, device_id=(row, (col + d) % n_col), device_id_type=MESH)
+    has_below, has_above = col > 0, col < n_col - 1
+
+    @pl.when(has_below)
+    def _():
+        pl.semaphore_signal(barrier, inc=1, device_id=(row, col - 1), device_id_type=MESH)
+
+    @pl.when(has_above)
+    def _():
+        pl.semaphore_signal(barrier, inc=1, device_id=(row, col + 1), device_id_type=MESH)
 
     @pl.when(col == 0)
     def _():
@@ -132,10 +140,9 @@
         landed[:, n_col] = jnp.zeros_like(landed[:, n_col])
 
     for h in range(halves):
-        for copy in mode_copies(False, start_ref, 0, h, 0):
+        for copy in mode_copies(h):
             copy.wait()
         gathered[h, row] = terms[0, h]
-    pl.semaphore_wait(barrier, chips + 2)
 
     def gather_copy(stage, slot, side, send, target):
         place = gathered.at[stage, slot] if side is None else gathered.at[stage, slot, side]
@@ -193,8 +200,6 @@
             return carry
 
         lax.fori_loop(0, 2 * len(indices), one, 0)
-
-    near = range(1, 3) if relay else range(1, chips)
 
     def gather_step(step, stage):
         if step == "gather":
@@ -354,11 +359,11 @@
             gathered[follower, row] = terms[k + 1, h]
 
     def prepare_chunk(index, carry):
-        slot = index % 2
-
-        @pl.when(index + 1 < chunks)
+        slot = index % ahead
+
+        @pl.when(index + ahead - 1 < chunks)
         def _():
-            for copy in fetch(index + 1, 1 - slot):
+            for copy in fetch(index + ahead - 1, (index + ahead - 1) % ahead):
                 copy.start()
 
         for copy in fetch(index, slot):
@@ -389,17 +394,20 @@
     def prepare(first, last):
         lax.fori_loop(chunks * first // 16, chunks * last // 16, prepare_chunk, 0)
 
+    prepare(0, 3)
+    beside = jnp.where(has_below, 1, 0) + jnp.where(has_above, 1, 0)
+    pl.semaphore_wait(barrier, len(near) + 1 + beside)
     gather_step("gather", 0)
-    prepare(0, 5)
+    prepare(3, 7)
     gather_step("relay", 0)
-    prepare(5, 9)
+    prepare(7, 10)
     gather_step("pass", 0)
     gather_step("fill near", 0)
     gather_step("gather", 1)
-    prepare(9, 12)
+    prepare(10, 11)
     gather_step("fill other", 0)
     gather_step("far", 0)
-    prepare(12, 14)
+    prepare(11, 12)
     gather_step("fill far", 0)
 
     def drain_gather(stage):
@@ -423,7 +431,7 @@
 
                 @pl.when(stage == 0)
                 def _():
-                    prepare(14, 16)
+                    prepare(12, 16)
 
             elif step == "drain":
                 drain_gather(stage)
@@ -454,39 +462,12 @@
 
     lax.fori_loop(0, stages, one_stage, 0)
     update(stages - 1)
-    outward = [(previous_ref, DEGREE - 1, 1), (filtered_ref, DEGREE, 2)]
-    for ref, degree, sem in outward:
-        for h in range(halves):
-            for copy in mode_copies(True, ref, degree, h, sem):
-                copy.start()
-
+    for h in range(halves):
+        for side in range(2):
+            here = (slice(h * part, (h + 1) * part), slice(side * side_len, (side + 1) * side_len))
+            filtered_ref[here] = terms[DEGREE, h, side]
+            previous_ref[here] = terms[DEGREE - 1, h, side]
     drain_shares(stages - 1)
-    for ref, degree, sem in outward:
-        for h in range(halves):
-            for copy in mode_copies(True, ref, degree, h, sem):
-                copy.wait()
-
-
-def hand_over(filtered_ref, previous_ref, filtered_out, previous_out, held, sems):
-    pieces = held.shape[1]
-    tall = held.shape[2]
-
-    def copies(inward):
-        both = []
-        for a, (ref, out) in enumerate(((filtered_ref, filtered_out), (previous_ref, previous_out))):
-            for p in range(pieces):
-                there, here = (ref if inward else out).at[pl.ds(p * tall, tall), :], held.at[a, p]
-                source, place = (there, here) if inward else (here, there)
-                both.append(pltpu.make_async_copy(source, place, sems.at[0 if inward else 1, a, p]))
-        return both
-
-    for copy in copies(True):
-        copy.start()
-    for came, goes in zip(copies(True), copies(False)):
-        came.wait()
-        goes.start()
-    for copy in copies(False):
-        copy.wait()
 
 
 def shards(start_modes, energies, coupling, pattern):
@@ -495,44 +476,36 @@
     per_piece = piece_len // BLOCK
     rows, slots, entries = coupling.shape
     pairs = (slots + 1) // 2
-    chunk, halves = min(16, per_piece), 2
+    ahead, chunk, halves = 4, min(8, per_piece), 2
     part, side_len = modes // halves, piece_len // 2
     stages = DEGREE * halves
     tall = entries // LANES
     by_slot = jnp.transpose(coupling, (1, 0, 2)).reshape(slots, rows // SUBLANES, SUBLANES, tall, LANES)
     vmem = pl.BlockSpec(memory_space=pltpu.VMEM)
     anywhere = pl.BlockSpec(memory_space=pl.ANY)
-    filtered, previous = pl.pallas_call(
+    return pl.pallas_call(
         functools.partial(filter_kernel, slots, n_row, n_col, halves),
         in_specs=[pl.BlockSpec(memory_space=pltpu.SMEM), anywhere, vmem, anywhere],
-        out_specs=[anywhere, anywhere],
-        out_shape=[jax.ShapeDtypeStruct(start_modes.shape, jnp.float32)] * 2,
+        out_specs=[vmem, vmem],
+        out_shape=[pltpu.VMEM(start_modes.shape, jnp.float32)] * 2,
         scratch_shapes=[
-            pltpu.VMEM((2, slots, chunk // SUBLANES, SUBLANES, tall, LANES), jnp.float32),
+            pltpu.VMEM((ahead, slots, chunk // SUBLANES, SUBLANES, tall, LANES), jnp.float32),
             pltpu.VMEM((rows, 2 * BLOCK, pairs * LANES), jnp.bfloat16),
             pltpu.VMEM((stages, n_row, 2, part, side_len), jnp.float32),
             pltpu.VMEM((halves, n_row * per_piece, 2 * part, LANES), jnp.bfloat16),
             pltpu.VMEM((DEGREE + 1, halves, 2, part, side_len), jnp.float32),
             pltpu.VMEM((stages, n_col, 2, part, side_len), jnp.float32),
             pltpu.VMEM((stages, n_col + 1, 2, part, side_len), jnp.float32),
-            pltpu.SemaphoreType.DMA((2, slots, SUBLANES)),
-            pltpu.SemaphoreType.DMA((3, halves, 2)),
+            pltpu.SemaphoreType.DMA((ahead, SUBLANES)),
+            pltpu.SemaphoreType.DMA((halves, 2)),
             pltpu.SemaphoreType.DMA((stages, max(10, n_row))),
             pltpu.SemaphoreType.DMA((stages, 2 * n_row)),
             pltpu.SemaphoreType.DMA((stages, 2 * n_col)),
             pltpu.SemaphoreType.DMA((stages, 2 * (n_col + 1))),
         ],
-        compiler_params=pltpu.CompilerParams(collective_id=0, has_side_effects=True, vmem_limit_bytes=67043328),
+        compiler_params=pltpu.CompilerParams(collective_id=0, has_side_effects=True, vmem_limit_bytes=65929216),
         name="filter",
     )(pattern.T, start_modes, energies.reshape(2, 1, side_len), jnp.transpose(by_slot, (0, 1, 3, 2, 4)))
-    return pl.pallas_call(
-        hand_over,
-        in_specs=[anywhere] * 2,
-        out_specs=[anywhere] * 2,
-        out_shape=[jax.ShapeDtypeStruct(start_modes.shape, jnp.float32)] * 2,
-        scratch_shapes=[pltpu.VMEM((2, modes // SUBLANES, SUBLANES, piece_len), jnp.float32), pltpu.SemaphoreType.DMA((2, 2, modes // SUBLANES))],
-        name="hand_over",
-    )(filtered, previous)
 
 
 def solution(mesh):

time: 134 us -> 130 us (0.970)
  Pallas kernels: 132 us -> 127 us
  local copies, waits for them, and re-layouts: 0 us -> 1.59 us
    pallas_call x1, Pallas kernels: 130 us -> 127 us  [shards(): pl.pallas_call(functools.partial(filter_kernel, slots, n_row, n_col, halv...]
    pallas_call x1 -> x0, Pallas kernels: 2.09 us -> none  [shards(): pl.pallas_call(hand_over, in_specs=[anywhere] * 2, out_specs=[anywhere] *...]
    unnamed x0 -> x2, local copies, waits for them, and re-layouts: none -> 1.59 us
where the time goes in v5:
time: 130 us; the launch traced here: 129 us
  Pallas kernels  127 us (98%)
  local copies, waits for them, and re-layouts  1.59 us (1%)
    pallas_call x1, Pallas kernels, shards(): pl.pallas_call(functools.partial(filter_kernel, slots, n_row, n_col, halv...  127 us

profile of v5, /device:TPU:0, one launch (start us, length us, event | category | flops | bytes accessed | tf_op | source)
XLA Modules:
  0.0 129.4 jit_solution(7684282790646081165)
XLA Ops:
  0.6 127.2 %filter.1 = (f32[32,4096]{1,0:T(8,128)S(1)}, f32[32,4096]{1,0:T(8,128)S(1)}) custom-call(s32[5,256]{1,0:T(8,128)} %bitcast.9, f32[32,4096]{1,0:T(8,128)} %start_ref.1, f32[2,1,2048]{2,1,0:T(1,128)} %bitcast.8, f32[5,32,32,8,128]{4,3,2,1,0:T(8,128)} %bitcast.7), custom_call_target="tpu_custom_call" | custom-call | tf_op jit(solution)/shard_map/filter/pallas_call | solution.py:486
  127.8 0.8 copy.8
  128.6 0.8 copy.9

commit v6 on v5

--- a/solution.py
+++ b/solution.py
@@ -30,12 +30,12 @@
         return (
             ("compute", 0, 2), ("update",), ("gather",), ("forward", 0, 1), ("compute", 2, 4), ("forward", 1, 2),
             ("compute", 4, 5), ("forward", 4, 5), ("relay",), ("forward", 2, 3), ("compute", 5, 6), ("pass",),
-            ("fill near",), ("forward", 5, 6), ("forward", 3, 4), ("prepare",), ("compute", 6, 7), ("fill other",),
+            ("fill near",), ("forward", 5, 6), ("forward", 3, 4), ("prepare", 14, 16), ("compute", 6, 7), ("fill other",),
             ("far",), ("compute", 7, 8), ("drain",), ("fill far",),
         )
     others = 2 * (n_col - 1)
     return (
-        ("compute", 0, 2), ("update",), ("gather",), ("prepare",), ("compute", 2, others), ("relay",), ("pass",), ("fill near",),
+        ("compute", 0, 2), ("update",), ("gather",), ("prepare", 14, 16), ("compute", 2, others), ("relay",), ("pass",), ("fill near",),
         ("forward", 0, others), ("compute", others, others + 2), ("fill other",), ("far",), ("drain",), ("fill far",),
     )
 
@@ -394,20 +394,20 @@
     def prepare(first, last):
         lax.fori_loop(chunks * first // 16, chunks * last // 16, prepare_chunk, 0)
 
-    prepare(0, 3)
+    prepare(0, 2)
     beside = jnp.where(has_below, 1, 0) + jnp.where(has_above, 1, 0)
     pl.semaphore_wait(barrier, len(near) + 1 + beside)
     gather_step("gather", 0)
-    prepare(3, 7)
+    prepare(2, 7)
     gather_step("relay", 0)
     prepare(7, 10)
     gather_step("pass", 0)
     gather_step("fill near", 0)
     gather_step("gather", 1)
-    prepare(10, 11)
+    prepare(10, 12)
     gather_step("fill other", 0)
     gather_step("far", 0)
-    prepare(11, 12)
+    prepare(12, 14)
     gather_step("fill far", 0)
 
     def drain_gather(stage):
@@ -420,6 +420,10 @@
             return carry
 
         lax.fori_loop(0, 2 * (n_col - 1), one, 0)
+
+    def put_out(ref, degree, h):
+        for side in range(2):
+            ref[h * part : (h + 1) * part, side * side_len : (side + 1) * side_len] = terms[degree, h, side]
 
     def one_stage(stage, carry):
         for step, *span in schedule(n_col):
@@ -431,10 +435,17 @@
 
                 @pl.when(stage == 0)
                 def _():
-                    prepare(12, 16)
+                    prepare(*span)
 
             elif step == "drain":
                 drain_gather(stage)
+
+                @pl.when(stage == stages - 1)
+                def _():
+                    for h in range(halves):
+                        put_out(previous_ref, DEGREE - 1, h)
+                    for h in range(halves - 1):
+                        put_out(filtered_ref, DEGREE, h)
 
                 @pl.when(stage > 0)
                 def _():
@@ -462,11 +473,7 @@
 
     lax.fori_loop(0, stages, one_stage, 0)
     update(stages - 1)
-    for h in range(halves):
-        for side in range(2):
-            here = (slice(h * part, (h + 1) * part), slice(side * side_len, (side + 1) * side_len))
-            filtered_ref[here] = terms[DEGREE, h, side]
-            previous_ref[here] = terms[DEGREE - 1, h, side]
+    put_out(filtered_ref, DEGREE, halves - 1)
     drain_shares(stages - 1)
 
 

time: 130 us -> 129 us (level)
  no operation moved by 1% of the time
where the time goes in v6:
time: 129 us
  Pallas kernels  127 us (98%)
  local copies, waits for them, and re-layouts  1.59 us (1%)
    pallas_call x1, Pallas kernels, shards(): pl.pallas_call(functools.partial(filter_kernel, slots, n_row, n_col, halv...  127 us

profile of v6, /device:TPU:0, one launch (start us, length us, event | category | flops | bytes accessed | tf_op | source)
XLA Modules:
  0.0 128.7 jit_solution(8841467396091130757)
XLA Ops:
  0.6 126.5 %filter.1 = (f32[32,4096]{1,0:T(8,128)S(1)}, f32[32,4096]{1,0:T(8,128)S(1)}) custom-call(s32[5,256]{1,0:T(8,128)} %bitcast.9, f32[32,4096]{1,0:T(8,128)} %start_ref.1, f32[2,1,2048]{2,1,0:T(1,128)} %bitcast.8, f32[5,32,32,8,128]{4,3,2,1,0:T(8,128)} %bitcast.7), custom_call_target="tpu_custom_call" | custom-call | tf_op jit(solution)/shard_map/filter/pallas_call | solution.py:493
  127.1 0.8 copy.8
  127.9 0.8 copy.9

commit v7 on v6

--- a/solution.py
+++ b/solution.py
@@ -55,7 +55,7 @@
     per_side = side_len // BLOCK
     per_piece = 2 * per_side
     rows = prepared.shape[0]
-    group = min(16, per_side)
+    group = min(32, per_side)
     pairs = (slots + 1) // 2
     stages = DEGREE * halves
     relay = chips == 4

time: 129 us -> 128 us (level)
  Pallas kernels: 127 us -> 125 us
where the time goes in v7:
time: 128 us
  Pallas kernels  125 us (98%)
  local copies, waits for them, and re-layouts  1.59 us (1%)
    pallas_call x1, Pallas kernels, shards(): pl.pallas_call(functools.partial(filter_kernel, slots, n_row, n_col, halv...  125 us

profile of v7, /device:TPU:0, one launch (start us, length us, event | category | flops | bytes accessed | tf_op | source)
XLA Modules:
  0.0 127.6 jit_solution(5792417656714876942)
XLA Ops:
  0.6 125.4 %filter.1 = (f32[32,4096]{1,0:T(8,128)S(1)}, f32[32,4096]{1,0:T(8,128)S(1)}) custom-call(s32[5,256]{1,0:T(8,128)} %bitcast.9, f32[32,4096]{1,0:T(8,128)} %start_ref.1, f32[2,1,2048]{2,1,0:T(1,128)} %bitcast.8, f32[5,32,32,8,128]{4,3,2,1,0:T(8,128)} %bitcast.7), custom_call_target="tpu_custom_call" | custom-call | tf_op jit(solution)/shard_map/filter/pallas_call | solution.py:493
  126.0 0.8 copy.8
  126.8 0.8 copy.9
